TPU v7x, 32 devices: a whole 2x2x4 slice. The times are simulated.
32 devices in a mesh: group: 4 (over y, x), shard: 8 (over z, core).
Axes of the slice: x: 2, y: 2, z: 4, core: 2. Of those that a mesh axis runs over, the one named last changes fastest.
Arguments:
- entity: float32 [16384, 400], P(('group', 'shard')), may hold values from -6 to 6
- entity_state: float32 [16384], P(('group', 'shard')), may hold values from 0.1 to 10
- relation: float32 [1345, 400], replicated, may hold values from -6 to 6
- relation_state: float32 [1345], replicated, may hold values from 10 to 1000
- src_send: int32 [32, 8, 128], P(('group', 'shard')), may hold values from 0 to 511
- dst_send: int32 [32, 8, 128], P(('group', 'shard')), may hold values from 0 to 511
- edge_source: int32 [32768], P(('group', 'shard')), may hold values from 0 to 1023
- edge_relation: int32 [32768], P(('group', 'shard')), may hold values from 0 to 1344
- edge_target: int32 [32768], P(('group', 'shard')), may hold values from 0 to 1023
- neg_slots: int32 [64, 1000], P(('group', 'shard')), may hold values from 0 to 1023
- edge_count: int32 [32], P(('group', 'shard')), may hold values from 1 to 1024, 10922 in all
Outputs:
- entity_new: float32 [16384, 400], P(('group', 'shard'))
- relation_new: float32 [1345, 400], replicated
- edge_loss: float32 [32768], P(('group', 'shard'))
Inputs may be any that keep to these rules, and one draw needn't show every extreme that they name: The live edges of a device are its first edge_count slots; some device has all 1024 live.
All inputs are finite; a program needn't handle non-finite values.
Results may differ from a plain program's by a relative error of at most 0.0003.
Values sent between devices are 32-bit elements; how exact they have to be, the bound alone decides.
No kernel may reach another device: no remote copies, remote signals or barrier semaphores. Data moves between devices by JAX's collectives and lax.ppermute only.
A program may use at most 128 MiB of HBM per device.

v0:
```python
import jax
import jax.numpy as jnp
from jax import lax
from jax.sharding import PartitionSpec as P

SPAN = 512
learn_rate = 0.5


def passed_along(value, axis, by):
    count = lax.axis_size(axis)
    return lax.ppermute(value, axis, [(i, (i + by) % count) for i in range(count)])


def complex_product(multiplier, multiplicand):
    half_width = multiplier.shape[1] // 2
    first_real, first_imag = (multiplier[:, :half_width], multiplier[:, half_width:])
    second_real, second_imag = (multiplicand[:, :half_width], multiplicand[:, half_width:])
    return jnp.concatenate(
        [
            first_real * second_real - first_imag * second_imag,
            first_real * second_imag + first_imag * second_real,
        ],
        axis=1,
    )


def conj_product(multiplier, multiplicand):
    half_width = multiplier.shape[1] // 2
    first_real, first_imag = (multiplier[:, :half_width], multiplier[:, half_width:])
    second_real, second_imag = (multiplicand[:, :half_width], multiplicand[:, half_width:])
    return jnp.concatenate(
        [
            first_real * second_real + first_imag * second_imag,
            first_imag * second_real - first_real * second_imag,
        ],
        axis=1,
    )


def span_terms(queries, tail_rows, negatives, live_mask):
    pos_score = jnp.sum(queries * tail_rows, axis=1)
    neg_score = jnp.dot(queries, negatives.T, precision=lax.Precision.HIGHEST)
    score_peak = jnp.maximum(pos_score, jnp.max(neg_score, axis=1))
    exp_total = jnp.exp(pos_score - score_peak) + jnp.sum(
        jnp.exp(neg_score - score_peak[:, None]), axis=1
    )
    log_total = score_peak + jnp.log(exp_total)
    edge_loss = (log_total - pos_score) * live_mask
    pos_grad = (jnp.exp(pos_score - log_total) - 1.0) * live_mask
    neg_grad = jnp.exp(neg_score - log_total[:, None]) * live_mask[:, None]
    neg_query = jnp.dot(neg_grad, negatives, precision=lax.Precision.HIGHEST)
    negative_grad = lax.dot_general(
        neg_grad, queries, (((0,), (0,)), ((), ())), precision=lax.Precision.HIGHEST
    )
    return (edge_loss, pos_grad, neg_query, negative_grad)


def adagrad(params, accumulator, gradient):
    new_state = accumulator + jnp.mean(gradient * gradient, axis=1)
    return params - learn_rate * gradient / jnp.sqrt(new_state)[:, None]


def on_device(
    entity,
    entity_state,
    relation,
    relation_state,
    src_send,
    dst_send,
    edge_source,
    edge_relation,
    edge_target,
    neg_slots,
    edge_count,
):
    feature_count = entity.shape[1]
    peer_count, block_size = (src_send.shape[1], src_send.shape[2])
    table_rows = peer_count * block_size
    edge_rows = edge_source.shape[0]
    spans = edge_rows // SPAN
    sent_source = lax.all_to_all(
        entity[src_send[0]], "shard", split_axis=0, concat_axis=0, tiled=True
    )
    source_table = sent_source.reshape(table_rows, feature_count)
    shifted = passed_along(entity[dst_send[0]], "group", -1)
    target_blocks = lax.all_to_all(shifted, "shard", split_axis=0, concat_axis=0, tiled=True)
    target_table = target_blocks.reshape(table_rows, feature_count)
    live_count = edge_count[0]
    live_mask = (jnp.arange(edge_rows, dtype=jnp.int32) < live_count).astype(jnp.float32)
    head_rows = source_table[edge_source]
    tail_rows = target_table[edge_target]
    rel_rows = relation[edge_relation]
    queries = complex_product(head_rows, rel_rows)

    def span_turn(position, carried):
        loss_all, pos_all, query_all, target_grad = carried
        first_row = position * SPAN
        slots = neg_slots[position]
        edge_loss, pos_grad, neg_query, negative_grad = span_terms(
            lax.dynamic_slice_in_dim(queries, first_row, SPAN),
            lax.dynamic_slice_in_dim(tail_rows, first_row, SPAN),
            target_table[slots],
            lax.dynamic_slice_in_dim(live_mask, first_row, SPAN),
        )
        loss_all = lax.dynamic_update_slice_in_dim(loss_all, edge_loss, first_row, 0)
        pos_all = lax.dynamic_update_slice_in_dim(pos_all, pos_grad, first_row, 0)
        query_all = lax.dynamic_update_slice_in_dim(query_all, neg_query, first_row, 0)
        target_grad = target_grad.at[slots].add(negative_grad)
        return (loss_all, pos_all, query_all, target_grad)

    initial = (
        jnp.zeros((edge_rows,), jnp.float32),
        jnp.zeros((edge_rows,), jnp.float32),
        jnp.zeros((edge_rows, feature_count), jnp.float32),
        jnp.zeros((table_rows, feature_count), jnp.float32),
    )
    edge_loss, pos_grad, neg_query, target_grad = lax.fori_loop(0, spans, span_turn, initial)
    query_grad = pos_grad[:, None] * tail_rows + neg_query
    target_grad = target_grad.at[edge_target].add(pos_grad[:, None] * queries)
    source_grad = (
        jnp.zeros((table_rows, feature_count), jnp.float32)
        .at[edge_source]
        .add(conj_product(query_grad, rel_rows))
    )
    relation_part = (
        jnp.zeros(relation.shape, jnp.float32)
        .at[edge_relation]
        .add(conj_product(query_grad, head_rows))
    )
    relation_total = lax.psum(relation_part, ("group", "shard"))
    returned_source = lax.all_to_all(
        source_grad.reshape(peer_count, block_size, feature_count),
        "shard",
        split_axis=0,
        concat_axis=0,
        tiled=True,
    )
    entity_grad = (
        jnp.zeros(entity.shape, jnp.float32)
        .at[src_send[0].reshape(-1)]
        .add(returned_source.reshape(-1, feature_count))
    )
    target_blocks_grad = target_grad.reshape(peer_count, block_size, feature_count)
    returned_blocks = lax.all_to_all(
        target_blocks_grad, "shard", split_axis=0, concat_axis=0, tiled=True
    )
    home_blocks = passed_along(returned_blocks, "group", 1)
    entity_grad = entity_grad.at[dst_send[0].reshape(-1)].add(
        home_blocks.reshape(-1, feature_count)
    )
    return (
        adagrad(entity, entity_state, entity_grad),
        adagrad(relation, relation_state, relation_total),
        edge_loss,
    )


def solution(mesh):
    return jax.shard_map(
        on_device,
        mesh=mesh,
        in_specs=(
            P(("group", "shard"), None),
            P(("group", "shard")),
            P(),
            P(),
            P(("group", "shard"), None, None),
            P(("group", "shard"), None, None),
            P(("group", "shard")),
            P(("group", "shard")),
            P(("group", "shard")),
            P(("group", "shard"), None),
            P(("group", "shard")),
        ),
        out_specs=(P(("group", "shard"), None), P(), P(("group", "shard"))),
        check_vma=False,
    )
```

profile of v0, /device:TPU:0, one launch (start us, length us, event | category | flops | bytes accessed | tf_op | source)
XLA Modules:
  0.0 453.2 jit_solution(17644259954135910867)
XLA Ops:
  9.4 3.5 gather_fusion.1
  12.9 1.7 copy.47
  14.6 6.5 %all-to-all-start = ((f32[8,128,400]{1,2,0:T(8,128)}), f32[8,128,400]{1,2,0:T(8,128)}, u32[]{:S(2)}, u32[]{:S(2)}) async-start(f32[8,128,400]{1,2,0:T(8,128)} %copy.47), calls=%async_computation | async-start | bytes 3276800 | tf_op jit(solution)/shard_map/all_to_all | solution.py:82
  21.1 3.5 gather_fusion.4
  24.6 1.8 copy.51
  26.4 2.4 collective-permute-start
  28.8 36.1 %collective-permute-done = f32[8,128,400]{1,2,0:T(8,128)} collective-permute-done((f32[8,128,400]{1,2,0:T(8,128)}, f32[8,128,400]{1,2,0:T(8,128)}, u32[]{:S(2)}, u32[]{:S(2)}) %collective-permute-start) | collective-permute-done | bytes 1638432 | tf_op jit(solution)/shard_map/ppermute | solution.py:12
  64.9 4.7 %all-to-all-start.1 = ((f32[8,128,400]{1,2,0:T(8,128)}), f32[8,128,400]{1,2,0:T(8,128)}, u32[]{:S(2)}, u32[]{:S(2)}) async-start(f32[8,128,400]{1,2,0:T(8,128)} %collective-permute-done), calls=%async_computation.1 | async-start | bytes 3276800 | tf_op jit(solution)/shard_map/all_to_all | solution.py:87
  69.6 2.5 copy.49
  72.9 4.9 %gather_fusion.3 = f32[1024,400]{1,0:T(8,128)} fusion(f32[1345,400]{1,0:T(8,128)S(1)} %copy.49, s32[1024]{0:T(1024)S(1)} %get-tuple-element.335), kind=kCustom, calls=%fused_computation.3 | custom fusion | bytes 3280896 | tf_op jit(solution)/shard_map/gather | solution.py:93
  77.8 1.8 copy.48
  79.6 4.9 %gather_fusion.2 = f32[1024,400]{1,0:T(8,128)} fusion(f32[1024,400]{1,0:T(8,128)S(1)} %bitcast.42, s32[1024]{0:T(1024)S(1)} %get-tuple-element.338), kind=kCustom, calls=%fused_computation.2 | custom fusion | bytes 3280896 | tf_op jit(solution)/shard_map/gather | solution.py:91
  84.6 3.1 multiply_subtract_fusion.2
  88.7 1.8 pad_maximum_fusion
  90.5 18.4 %all-to-all-done.1 = f32[8,128,400]{1,2,0:T(8,128)} async-done(((f32[8,128,400]{1,2,0:T(8,128)}), f32[8,128,400]{1,2,0:T(8,128)}, u32[]{:S(2)}, u32[]{:S(2)}) %all-to-all-start.1) | async-done | bytes 1638432 | tf_op jit(solution)/shard_map/all_to_all | solution.py:87
  108.9 1.8 copy.52
  110.8 4.9 %gather_fusion.5 = f32[1024,400]{1,0:T(8,128)} fusion(f32[1024,400]{1,0:T(8,128)S(1)} %bitcast.39, s32[1024]{0:T(1024)S(1)} %get-tuple-element.337), kind=kCustom, calls=%fused_computation.5 | custom fusion | bytes 3280896 | tf_op jit(solution)/shard_map/gather | solution.py:92
  118.7 68.8 %while.21 = (s32[]{:T(128)}, f32[1024]{0:T(1024)S(1)}, f32[1024]{0:T(1024)S(1)}, f32[1024,400]{0,1:T(8,128)}, f32[1024,400]{1,0:T(8,128)}, /*index=5*/f32[1024,4...) while((s32[]{:T(128)}, f32[1024]{0:T(1024)S(1)}, ...), condition=%wide.region_5.0_spmd, body=%wide.region_0.0_spmd.sunk | while | flops 7377200640 | bytes 52573032 | solution.py:118
  120.9 4.9 %gather_fusion = f32[1000,400]{1,0:T(8,128)} fusion(f32[1024,400]{1,0:T(8,128)S(1)} %get-tuple-element.447, s32[1024]{0:T(1024)S(1)} %pad_clamp_fusion.2), kind=kCustom, calls=%fused_computation.clone.1 | custom fusion | bytes 3204000 | tf_op jit(solution)/shard_map/while/body/eval_jaxpr/gather | solution.py:103
  125.8 5.4 %fusion.44 = (f32[512]{0:T(512)S(1)}, f32[512,1000]{0,1:T(8,128)S(1)}) fusion(f32[1000,400]{1,0:T(8,128)} %gather_fusion, f32[1024,400]{1,0:T(8,128)} %get-tuple-element.444, s32[]{:T(128)S(6)} %select_n.125), kind=kOutput, calls=%fused_computation.77.clone.1 | convolution fusion | flops 2458111488 | bytes 5146628 | tf_op jit(solution)/shard_map/while/body/eval_jaxpr/dot_general | solution.py:43
  132.8 4.2 fusion.45
  138.3 4.9 %fusion.46 = f32[1000,400]{1,0:T(8,128)} fusion(f32[512,1000]{0,1:T(8,128)S(1)} %get-tuple-element.407, f32[512]{0:T(512)S(1)} %get-tuple-element.408, f32[512]{0:T(512)S(1)} %get-tuple-element.409, f32[1024,400]{1,0:T(8,128)S(1)} %copy-done.5, s32[]{:T(128)S(6)} %select_n.125), kind=kOutput, calls=%fused_computation.14.clone.1 | convolution fusion | flops 2458624000 | bytes 4700676 | tf_op jit(solution)/shard_map/while/body/eval_jaxpr/dot_general | solution.py:53
  143.2 10.1 %scatter_fusion = f32[1024,400]{1,0:T(8,128)} fusion(f32[1024,400]{1,0:T(8,128)} %get-tuple-element.429, s32[1000]{0:T(1024)S(1)} %bitcast.49, f32[1000,400]{1,0:T(8,128)} %fusion.46), kind=kCustom, calls=%fused_computation.6.clone.1 | custom fusion | flops 400000 | bytes 4804000 | tf_op jit(solution)/shard_map/while/body/eval_jaxpr/scatter-add | solution.py:109
  155.0 4.9 %gather_fusion = f32[1000,400]{1,0:T(8,128)} fusion(f32[1024,400]{1,0:T(8,128)S(1)} %get-tuple-element.447, s32[1024]{0:T(1024)S(1)} %pad_clamp_fusion.2), kind=kCustom, calls=%fused_computation.clone.1 | custom fusion | bytes 3204000 | tf_op jit(solution)/shard_map/while/body/eval_jaxpr/gather | solution.py:103
  159.9 5.4 %fusion.44 = (f32[512]{0:T(512)S(1)}, f32[512,1000]{0,1:T(8,128)S(1)}) fusion(f32[1000,400]{1,0:T(8,128)} %gather_fusion, f32[1024,400]{1,0:T(8,128)} %get-tuple-element.444, s32[]{:T(128)S(6)} %select_n.125), kind=kOutput, calls=%fused_computation.77.clone.1 | convolution fusion | flops 2458111488 | bytes 5146628 | tf_op jit(solution)/shard_map/while/body/eval_jaxpr/dot_general | solution.py:43
  166.9 4.2 fusion.45
  172.4 4.9 %fusion.46 = f32[1000,400]{1,0:T(8,128)} fusion(f32[512,1000]{0,1:T(8,128)S(1)} %get-tuple-element.407, f32[512]{0:T(512)S(1)} %get-tuple-element.408, f32[512]{0:T(512)S(1)} %get-tuple-element.409, f32[1024,400]{1,0:T(8,128)S(1)} %copy-done.5, s32[]{:T(128)S(6)} %select_n.125), kind=kOutput, calls=%fused_computation.14.clone.1 | convolution fusion | flops 2458624000 | bytes 4700676 | tf_op jit(solution)/shard_map/while/body/eval_jaxpr/dot_general | solution.py:53
  177.2 10.1 %scatter_fusion = f32[1024,400]{1,0:T(8,128)} fusion(f32[1024,400]{1,0:T(8,128)} %get-tuple-element.429, s32[1000]{0:T(1024)S(1)} %bitcast.49, f32[1000,400]{1,0:T(8,128)} %fusion.46), kind=kCustom, calls=%fused_computation.6.clone.1 | custom fusion | flops 400000 | bytes 4804000 | tf_op jit(solution)/shard_map/while/body/eval_jaxpr/scatter-add | solution.py:109
  187.5 10.6 %scatter_custom_fusion.3 = f32[1024,400]{1,0:T(8,128)} fusion(f32[1024,400]{1,0:T(8,128)} %get-tuple-element.250, s32[1024]{0:T(1024)S(1)} %get-tuple-element.336, f32[1024]{0:T(1024)S(1)} %get-tuple-element.248, f32[1024,200]{1,0:T(8,128)} %copy-done.9, f32[1024,200]{1,0:T(8,128)S(1)} %get-tuple-element.330), kind=kCustom, calls=%fused_computation.43 | custom fusion | flops 1228800 | bytes 3739648 | tf_op jit(solution)/shard_map/scatter-add | solution.py:120
  198.1 2.8 copy.59
  200.9 4.3 all-to-all-start.3
  205.2 3.0 copy.54
  208.2 2.0 multiply_add_fusion
  211.0 2.5 multiply_add_fusion.1
  213.6 8.1 %scatter_custom_fusion.1 = f32[1024,400]{1,0:T(8,128)S(1)} fusion(s32[1024]{0:T(1024)S(1)} %get-tuple-element.339, f32[1024,200]{1,0:T(8,128)S(1)} %get-tuple-element.332, f32[]{:T(128)} %constant.108, f32[1024,200]{1,0:T(8,128)} %get-tuple-element.333, f32[]{:T(128)} %constant.97.clone.1), kind=kCustom, calls=%fused_computation.35 | custom fusion | flops 819200 | bytes 3506184 | tf_op jit(solution)/shard_map/scatter-add | solution.py:124
  221.7 1.7 copy.55
  223.5 21.0 %all-to-all-done.3 = f32[8,128,400]{1,2,0:T(8,128)} async-done(((f32[8,128,400]{1,2,0:T(8,128)}), f32[8,128,400]{1,2,0:T(8,128)}, u32[]{:S(2)}, u32[]{:S(2)}) %all-to-all-start.3) | async-done | bytes 1638432 | tf_op jit(solution)/shard_map/all_to_all | solution.py:145
  244.4 4.3 all-to-all-start.2
  248.8 9.0 %scatter_custom_fusion.5 = f32[1345,400]{1,0:T(8,128)} fusion(s32[1024]{0:T(1024)S(1)} %get-tuple-element.334, f32[1024,200]{1,0:T(8,128)S(1)} %copy-done.13, f32[]{:T(128)} %constant.108, f32[1024,200]{1,0:T(8,128)S(1)} %copy-done.12, f32[]{:T(128)} %constant.97.clone.1), kind=kCustom, calls=%fused_computation.39 | custom fusion | flops 819200 | bytes 4249160 | tf_op jit(solution)/shard_map/scatter-add | solution.py:129
  257.8 2.4 collective-permute-start.1
  260.3 155.8 %all-reduce.2.cloned.1.call-done = f32[1345,400]{1,0:T(8,128)} async-done(((f32[1345,400]{1,0:T(8,128)}), f32[1345,400]{1,0:T(8,128)}) %all-reduce.2.cloned.1.call-update) | async-done | bytes 2152016 | tf_op jit(solution)/shard_map/psum | solution.py:131
  416.1 2.1 multiply_reduce_fusion.1
  418.2 3.8 divide_subtract_fusion
  422.0 3.3 copy.65
  425.3 1.8 copy.67
  427.1 6.8 %scatter_custom_fusion.2 = f32[512,400]{1,0:T(8,128)S(1)} fusion(s32[1024]{0:T(1024)S(1)} %bitcast.53, f32[1024,400]{1,0:T(8,128)S(1)} %bitcast.47, f32[]{:T(128)} %constant.97.clone.1), kind=kCustom, calls=%fused_computation.57 | custom fusion | flops 409600 | bytes 819204 | tf_op jit(solution)/shard_map/scatter-add | solution.py:142
  434.0 2.8 copy.70
  436.8 7.8 %scatter_fusion.1 = f32[512,400]{1,0:T(8,128)S(1)} fusion(f32[512,400]{1,0:T(8,128)S(1)} %scatter_custom_fusion.2, s32[1024]{0:T(1024)S(1)} %bitcast.50, f32[1024,400]{1,0:T(8,128)} %bitcast.43), kind=kCustom, calls=%fused_computation.10 | custom fusion | flops 409600 | bytes 4919296 | tf_op jit(solution)/shard_map/scatter-add | solution.py:149
  (91 shorter events, 18.0 us)
Async XLA Ops:
  8.6 12.5 %copy-start = (f32[512,400]{1,0:T(8,128)}, f32[512,400]{1,0:T(8,128)S(1)}, u32[]{:S(2)}) copy-start(f32[512,400]{1,0:T(8,128)S(1)} %copy.62) | copy-start | bytes 2457604
  14.6 6.5 %copy-start.16 = (s32[1,8,128]{2,1,0:T(8,128)S(1)}, s32[1,8,128]{2,1,0:T(8,128)}, u32[]{:S(2)}) copy-start(s32[1,8,128]{2,1,0:T(8,128)} %param.18) | copy-start | bytes 12292
  14.6 50.3 %all-to-all-start = ((f32[8,128,400]{1,2,0:T(8,128)}), f32[8,128,400]{1,2,0:T(8,128)}, u32[]{:S(2)}, u32[]{:S(2)}) async-start(f32[8,128,400]{1,2,0:T(8,128)} %copy.47), calls=%async_computation | async-start | bytes 3276800 | tf_op jit(solution)/shard_map/all_to_all | solution.py:82
  26.4 38.5 %collective-permute-start = (f32[8,128,400]{1,2,0:T(8,128)}, f32[8,128,400]{1,2,0:T(8,128)}, u32[]{:S(2)}, u32[]{:S(2)}) collective-permute-start(f32[8,128,400]{1,2,0:T(8,128)} %copy.51), channel_id=1, source_target_pairs={{0,24},{8,0},{16,8},{24,16},{1,25},{9,1},{17,9},{25,17},{2,26},{10... | collective-permute-start | bytes 4915208 | tf_op jit(solution)/shard_map/ppermute | solution.py:12
  64.9 44.0 %all-to-all-start.1 = ((f32[8,128,400]{1,2,0:T(8,128)}), f32[8,128,400]{1,2,0:T(8,128)}, u32[]{:S(2)}, u32[]{:S(2)}) async-start(f32[8,128,400]{1,2,0:T(8,128)} %collective-permute-done), calls=%async_computation.1 | async-start | bytes 3276800 | tf_op jit(solution)/shard_map/all_to_all | solution.py:87
  69.6 3.2 copy-start.18
  72.1 5.6 %copy-start.3 = (f32[1345,400]{1,0:T(8,128)}, f32[1345,400]{1,0:T(8,128)S(1)}, u32[]{:S(2)}) copy-start(f32[1345,400]{1,0:T(8,128)S(1)} %copy.49) | copy-start | bytes 6456004
  72.8 4.9 %copy-start.19 = (s32[1024]{0:T(1024)S(1)}, s32[1024]{0:T(1024)}, u32[]{:S(2)}) copy-start(s32[1024]{0:T(1024)} %param.19) | copy-start | bytes 12292
  72.8 4.9 %copy-start.20 = (s32[1024]{0:T(1024)S(1)}, s32[1024]{0:T(1024)}, u32[]{:S(2)}) copy-start(s32[1024]{0:T(1024)} %param.21) | copy-start | bytes 12292
  87.7 1.0 copy-start.9
  115.6 3.1 copy-start.14
  125.8 6.1 %copy-start.10 = (f32[1024,400]{0,1:T(8,128)S(1)}, f32[1024,400]{0,1:T(8,128)}, u32[]{:S(2)}) copy-start(f32[1024,400]{0,1:T(8,128)} %get-tuple-element.428) | copy-start | bytes 4915204 | tf_op jit(solution)/shard_map/while
  131.2 1.6 copy-start.2
  132.8 5.5 %copy-start.5 = (f32[1024,400]{1,0:T(8,128)S(1)}, f32[1024,400]{1,0:T(8,128)}, u32[]{:S(2)}) copy-start(f32[1024,400]{1,0:T(8,128)} %get-tuple-element.444) | copy-start | bytes 4915204 | tf_op jit(solution)/shard_map/while
  137.0 1.3 copy-start.11
  159.9 6.1 %copy-start.10 = (f32[1024,400]{0,1:T(8,128)S(1)}, f32[1024,400]{0,1:T(8,128)}, u32[]{:S(2)}) copy-start(f32[1024,400]{0,1:T(8,128)} %get-tuple-element.428) | copy-start | bytes 4915204 | tf_op jit(solution)/shard_map/while
  165.3 1.6 copy-start.2
  166.9 5.5 %copy-start.5 = (f32[1024,400]{1,0:T(8,128)S(1)}, f32[1024,400]{1,0:T(8,128)}, u32[]{:S(2)}) copy-start(f32[1024,400]{1,0:T(8,128)} %get-tuple-element.444) | copy-start | bytes 4915204 | tf_op jit(solution)/shard_map/while
  171.1 1.3 copy-start.11
  187.5 10.6 %copy-start.21 = (f32[1024]{0:T(1024)}, f32[1024]{0:T(1024)S(1)}, u32[]{:S(2)}) copy-start(f32[1024]{0:T(1024)S(1)} %get-tuple-element.300) | copy-start | bytes 12292
  200.9 43.5 %all-to-all-start.3 = ((f32[8,128,400]{1,2,0:T(8,128)}), f32[8,128,400]{1,2,0:T(8,128)}, u32[]{:S(2)}, u32[]{:S(2)}) async-start(f32[8,128,400]{1,2,0:T(8,128)} %copy.59), calls=%async_computation.3 | async-start | bytes 3276800 | tf_op jit(solution)/shard_map/all_to_all | solution.py:145
  205.2 3.0 copy-start.6
  208.2 2.2 copy-start.7
  208.2 2.9 copy-start.8
  223.5 25.3 %copy-start.12 = (f32[1024,200]{1,0:T(8,128)S(1)}, f32[1024,200]{1,0:T(8,128)}, u32[]{:S(2)}) copy-start(f32[1024,200]{1,0:T(8,128)} %get-tuple-element.326) | copy-start | bytes 2457604
  223.5 25.3 %copy-start.13 = (f32[1024,200]{1,0:T(8,128)S(1)}, f32[1024,200]{1,0:T(8,128)}, u32[]{:S(2)}) copy-start(f32[1024,200]{1,0:T(8,128)} %get-tuple-element.327) | copy-start | bytes 2457604
  244.4 180.8 %all-to-all-start.2 = ((f32[8,128,400]{1,2,0:T(8,128)}), f32[8,128,400]{1,2,0:T(8,128)}, u32[]{:S(2)}, u32[]{:S(2)}) async-start(f32[8,128,400]{1,2,0:T(8,128)} %copy.55), calls=%async_computation.2 | async-start | bytes 3276800 | tf_op jit(solution)/shard_map/all_to_all | solution.py:132
  248.7 167.4 %all-reduce.2.cloned.1.call-start = ((), (), s32[]{:S(2)}) async-start(), calls=%async_computation.4 | async-start | bytes 5537792 | tf_op jit(solution)/shard_map/psum | solution.py:131
  257.8 2.5 copy-start.15
  257.8 160.4 %copy-start.17 = (f32[1345]{0:T(1024)S(1)}, f32[1345]{0:T(1024)}, u32[]{:S(2)}) copy-start(f32[1345]{0:T(1024)} %param.16) | copy-start | bytes 16144
  257.8 160.4 %copy-start.4 = (f32[1345,400]{1,0:T(8,128)S(1)}, f32[1345,400]{1,0:T(8,128)}, u32[]{:S(2)}) copy-start(f32[1345,400]{1,0:T(8,128)} %copy-done.3) | copy-start | bytes 6456004
  257.8 176.1 %collective-permute-start.1 = (f32[8,128,400]{1,2,0:T(8,128)}, f32[8,128,400]{1,2,0:T(8,128)}, u32[]{:S(2)}, u32[]{:S(2)}) collective-permute-start(f32[8,128,400]{1,2,0:T(8,128)} %all-to-all-done.3), channel_id=1, source_target_pairs={{0,8},{8,16},{16,24},{24,0},{1,9},{9,17},{17,25},{25,1},{2,10},{10... | collective-permute-start | bytes 4915208 | tf_op jit(solution)/shard_map/ppermute | solution.py:12
  436.8 7.9 %copy-start.22 = (f32[512]{0:T(512)S(1)}, f32[512]{0:T(512)}, u32[]{:S(2)}) copy-start(f32[512]{0:T(512)} %param.14) | copy-start | bytes 6148
  436.8 7.9 %copy-start.1 = (f32[512,400]{1,0:T(8,128)S(1)}, f32[512,400]{1,0:T(8,128)}, u32[]{:S(2)}) copy-start(f32[512,400]{1,0:T(8,128)} %copy-done) | copy-start | bytes 2457604
Sparse Core Ops, SparseCore 0:
  257.9 158.1 all-reduce.1
where the time goes:
time: 458 us; the launch traced here: 453 us
  waiting for transfers between devices  231 us (50%)
  other arithmetic  83.6 us (18%)
  local copies, waits for them, and re-layouts  68.6 us (15%)
  matrix products  29 us (6%)
  starting transfers between devices  24.7 us (5%)
  between operations  15.3 us (3%)
    psum x1, waiting for transfers between devices, on_device(): relation_total = lax.psum(relation_part, ('group', 'shard'))  156 us
    ppermute x2, waiting for transfers between devices, passed_along(): lax.ppermute(value, axis, [(i, (i + by) % count) for i in range(count)])  36.1 us
    all_to_all x1, waiting for transfers between devices, on_device(): lax.all_to_all(target_blocks_grad, 'shard', split_axis=0, concat_axis=0,...  21 us
    scatter-add x2, other arithmetic, span_turn(): target_grad = target_grad.at[slots].add(negative_grad)  20.2 us
    all_to_all x1, waiting for transfers between devices, on_device(): lax.all_to_all(shifted, 'shard', split_axis=0, concat_axis=0, tiled=True)  18.4 us
    dot_general x2, matrix products, span_terms(): neg_score = jnp.dot(queries, negatives.T, precision=lax.Precision.HIGHEST)  10.9 us
    scatter-add x1, other arithmetic, on_device(): target_grad = target_grad.at[edge_target].add(pos_grad[:, None] * queries)  10.6 us
    unnamed x42, local copies, waits for them, and re-layouts  10.4 us
  transfers between devices with their start and end apart: 7, of which 4 were waited for; matrix products, arithmetic and copies ran while one was open for 15% of the time, Pallas kernels for 0%

commit v1 on v0

--- a/solution.py
+++ b/solution.py
@@ -142,9 +142,22 @@
         .add(returned_source.reshape(-1, feature_count))
     )
     target_blocks_grad = target_grad.reshape(peer_count, block_size, feature_count)
-    returned_blocks = lax.all_to_all(
-        target_blocks_grad, "shard", split_axis=0, concat_axis=0, tiled=True
-    )
+
+    def treat_the_shifts_all(inputs):
+        mesh_ax = "shard"
+        kept_arr, q_next = (lax.psum(1, mesh_ax), lax.axis_index(mesh_ax))
+        right_arr = inputs.shape[0] // kept_arr
+        even = jnp.roll(inputs, -q_next * right_arr, 0)
+        queue = [lax.slice_in_dim(even, 0, right_arr, axis=0)]
+        for j in range(1, kept_arr):
+            a_now = lax.slice_in_dim(even, j * right_arr, (j + 1) * right_arr, axis=0)
+            queue.append(
+                lax.ppermute(a_now, mesh_ax, [(w, (w + j) % kept_arr) for w in range(kept_arr)])
+            )
+        main = jnp.concatenate(queue[::-1], 0)
+        return jnp.roll(main, (q_next + 1) * queue[0].shape[0], 0)
+
+    returned_blocks = treat_the_shifts_all(target_blocks_grad)
     home_blocks = passed_along(returned_blocks, "group", 1)
     entity_grad = entity_grad.at[dst_send[0].reshape(-1)].add(
         home_blocks.reshape(-1, feature_count)

time: 458 us -> 462 us (level)
  waiting for transfers between devices: 231 us -> 200 us
  starting transfers between devices: 24.7 us -> 50.2 us
  local copies, waits for them, and re-layouts: 68.6 us -> 77.6 us
    psum x1, waiting for transfers between devices: 156 us -> 111 us  [on_device(): relation_total = lax.psum(relation_part, ('group', 'shard'))]
    ppermute x0 -> x7, waiting for transfers between devices: none -> 35.3 us  [treat_the_shifts_all(): lax.ppermute(a_now, mesh_ax, [(w, (w + j) % kept_arr) for w in range(kept...]
    ppermute x0 -> x7, starting transfers between devices: none -> 29.7 us  [treat_the_shifts_all(): lax.ppermute(a_now, mesh_ax, [(w, (w + j) % kept_arr) for w in range(kept...]
    all_to_all x1 -> x0, waiting for transfers between devices: 21 us -> none  [on_device(): lax.all_to_all(target_blocks_grad, 'shard', split_axis=0, concat_axis=0,...]
    concatenate x0 -> x1, local copies, waits for them, and re-layouts: none -> 6.13 us  [treat_the_shifts_all(): main = jnp.concatenate(queue[::-1], 0)]
    unnamed x42 -> x46, local copies, waits for them, and re-layouts: 10.4 us -> 11.9 us
  transfers between devices with their start and end apart: 7 -> 13, of which waited for: 4 -> 6; matrix products, arithmetic and copies ran while one was open for 15% -> 14% of each run, Pallas kernels for 0% -> 0%
where the time goes in v1:
time: 462 us; the launch traced here: 457 us
  waiting for transfers between devices  200 us (43%)
  other arithmetic  83.5 us (18%)
  local copies, waits for them, and re-layouts  77.6 us (17%)
  starting transfers between devices  50.2 us (11%)
  matrix products  29.2 us (6%)
  between operations  15.4 us (3%)
    psum x1, waiting for transfers between devices, on_device(): relation_total = lax.psum(relation_part, ('group', 'shard'))  111 us
    ppermute x2, waiting for transfers between devices, passed_along(): lax.ppermute(value, axis, [(i, (i + by) % count) for i in range(count)])  36.1 us
    ppermute x7, waiting for transfers between devices, treat_the_shifts_all(): lax.ppermute(a_now, mesh_ax, [(w, (w + j) % kept_arr) for w in range(kept...  35.3 us
    ppermute x7, starting transfers between devices, treat_the_shifts_all(): lax.ppermute(a_now, mesh_ax, [(w, (w + j) % kept_arr) for w in range(kept...  29.7 us
    scatter-add x2, other arithmetic, span_turn(): target_grad = target_grad.at[slots].add(negative_grad)  20.2 us
    all_to_all x1, waiting for transfers between devices, on_device(): lax.all_to_all(shifted, 'shard', split_axis=0, concat_axis=0, tiled=True)  18.4 us
    unnamed x46, local copies, waits for them, and re-layouts  11.9 us
    dot_general x2, matrix products, span_terms(): neg_score = jnp.dot(queries, negatives.T, precision=lax.Precision.HIGHEST)  10.9 us
  transfers between devices with their start and end apart: 13, of which 6 were waited for; matrix products, arithmetic and copies ran while one was open for 14% of the time, Pallas kernels for 0%

profile of v1, /device:TPU:0, one launch (start us, length us, event | category | flops | bytes accessed | tf_op | source)
XLA Modules:
  0.0 457.1 jit_solution(11899529721541960390)
XLA Ops:
  9.4 3.5 gather_fusion.1
  14.6 6.5 %all-to-all-start = ((f32[8,128,400]{1,2,0:T(8,128)}), f32[8,128,400]{1,2,0:T(8,128)}, u32[]{:S(2)}, u32[]{:S(2)}) async-start(f32[8,128,400]{1,2,0:T(8,128)} %copy.48), calls=%async_computation | async-start | bytes 3276800 | tf_op jit(solution)/shard_map/all_to_all | solution.py:82
  21.1 3.5 gather_fusion.4
  26.4 2.4 collective-permute-start
  28.9 36.1 %collective-permute-done = f32[8,128,400]{1,2,0:T(8,128)} collective-permute-done((f32[8,128,400]{1,2,0:T(8,128)}, f32[8,128,400]{1,2,0:T(8,128)}, u32[]{:S(2)}, u32[]{:S(2)}) %collective-permute-start) | collective-permute-done | bytes 1638432 | tf_op jit(solution)/shard_map/ppermute | solution.py:12
  64.9 4.7 %all-to-all-start.1 = ((f32[8,128,400]{1,2,0:T(8,128)}), f32[8,128,400]{1,2,0:T(8,128)}, u32[]{:S(2)}, u32[]{:S(2)}) async-start(f32[8,128,400]{1,2,0:T(8,128)} %collective-permute-done), calls=%async_computation.1 | async-start | bytes 3276800 | tf_op jit(solution)/shard_map/all_to_all | solution.py:87
  69.6 2.5 copy.50
  72.9 4.9 %gather_fusion.3 = f32[1024,400]{1,0:T(8,128)} fusion(f32[1345,400]{1,0:T(8,128)S(1)} %copy.50, s32[1024]{0:T(1024)S(1)} %get-tuple-element.344), kind=kCustom, calls=%fused_computation.3 | custom fusion | bytes 3280896 | tf_op jit(solution)/shard_map/gather | solution.py:93
  77.8 1.8 copy.49
  79.7 4.9 %gather_fusion.2 = f32[1024,400]{1,0:T(8,128)} fusion(f32[1024,400]{1,0:T(8,128)S(1)} %bitcast.42, s32[1024]{0:T(1024)S(1)} %get-tuple-element.347), kind=kCustom, calls=%fused_computation.2 | custom fusion | bytes 3280896 | tf_op jit(solution)/shard_map/gather | solution.py:91
  84.5 3.3 multiply_subtract_fusion.2
  90.6 18.4 %all-to-all-done.1 = f32[8,128,400]{1,2,0:T(8,128)} async-done(((f32[8,128,400]{1,2,0:T(8,128)}), f32[8,128,400]{1,2,0:T(8,128)}, u32[]{:S(2)}, u32[]{:S(2)}) %all-to-all-start.1) | async-done | bytes 1638432 | tf_op jit(solution)/shard_map/all_to_all | solution.py:87
  110.8 4.9 %gather_fusion.5 = f32[1024,400]{1,0:T(8,128)} fusion(f32[1024,400]{1,0:T(8,128)S(1)} %bitcast.39, s32[1024]{0:T(1024)S(1)} %get-tuple-element.346), kind=kCustom, calls=%fused_computation.5 | custom fusion | bytes 3280896 | tf_op jit(solution)/shard_map/gather | solution.py:92
  118.7 68.9 %while.21 = (s32[]{:T(128)}, f32[1024]{0:T(1024)S(1)}, f32[1024]{0:T(1024)S(1)}, f32[1024,400]{0,1:T(8,128)}, f32[1024,400]{1,0:T(8,128)}, /*index=5*/f32[1024,4...) while((s32[]{:T(128)}, f32[1024]{0:T(1024)S(1)}, ...), condition=%wide.region_5.0_spmd, body=%wide.region_0.0_spmd.sunk | while | flops 7377200640 | bytes 52573032 | solution.py:118
  121.0 4.9 %gather_fusion = f32[1000,400]{1,0:T(8,128)} fusion(f32[1024,400]{1,0:T(8,128)S(1)} %get-tuple-element.456, s32[1024]{0:T(1024)S(1)} %pad_clamp_fusion.2), kind=kCustom, calls=%fused_computation.clone.1 | custom fusion | bytes 3204000 | tf_op jit(solution)/shard_map/while/body/eval_jaxpr/gather | solution.py:103
  125.8 5.4 %fusion.47 = (f32[512]{0:T(512)S(1)}, f32[512,1000]{0,1:T(8,128)S(1)}) fusion(f32[1000,400]{1,0:T(8,128)} %gather_fusion, f32[1024,400]{1,0:T(8,128)} %get-tuple-element.453, s32[]{:T(128)S(6)} %select_n.141), kind=kOutput, calls=%fused_computation.83.clone.1 | convolution fusion | flops 2458111488 | bytes 5146628 | tf_op jit(solution)/shard_map/while/body/eval_jaxpr/dot_general | solution.py:43
  132.8 4.2 fusion.48
  138.2 5.0 %fusion.49 = f32[1000,400]{1,0:T(8,128)} fusion(f32[512,1000]{0,1:T(8,128)S(1)} %get-tuple-element.416, f32[512]{0:T(512)S(1)} %get-tuple-element.417, f32[512]{0:T(512)S(1)} %get-tuple-element.418, f32[1024,400]{1,0:T(8,128)S(1)} %copy-done.6, s32[]{:T(128)S(6)} %select_n.141), kind=kOutput, calls=%fused_computation.14.clone.1 | convolution fusion | flops 2458624000 | bytes 4700676 | tf_op jit(solution)/shard_map/while/body/eval_jaxpr/dot_general | solution.py:53
  143.2 10.1 %scatter_fusion = f32[1024,400]{1,0:T(8,128)} fusion(f32[1024,400]{1,0:T(8,128)} %get-tuple-element.438, s32[1000]{0:T(1024)S(1)} %bitcast.49, f32[1000,400]{1,0:T(8,128)} %fusion.49), kind=kCustom, calls=%fused_computation.6.clone.1 | custom fusion | flops 400000 | bytes 4804000 | tf_op jit(solution)/shard_map/while/body/eval_jaxpr/scatter-add | solution.py:109
  155.1 4.9 %gather_fusion = f32[1000,400]{1,0:T(8,128)} fusion(f32[1024,400]{1,0:T(8,128)S(1)} %get-tuple-element.456, s32[1024]{0:T(1024)S(1)} %pad_clamp_fusion.2), kind=kCustom, calls=%fused_computation.clone.1 | custom fusion | bytes 3204000 | tf_op jit(solution)/shard_map/while/body/eval_jaxpr/gather | solution.py:103
  159.9 5.4 %fusion.47 = (f32[512]{0:T(512)S(1)}, f32[512,1000]{0,1:T(8,128)S(1)}) fusion(f32[1000,400]{1,0:T(8,128)} %gather_fusion, f32[1024,400]{1,0:T(8,128)} %get-tuple-element.453, s32[]{:T(128)S(6)} %select_n.141), kind=kOutput, calls=%fused_computation.83.clone.1 | convolution fusion | flops 2458111488 | bytes 5146628 | tf_op jit(solution)/shard_map/while/body/eval_jaxpr/dot_general | solution.py:43
  166.9 4.2 fusion.48
  172.3 5.0 %fusion.49 = f32[1000,400]{1,0:T(8,128)} fusion(f32[512,1000]{0,1:T(8,128)S(1)} %get-tuple-element.416, f32[512]{0:T(512)S(1)} %get-tuple-element.417, f32[512]{0:T(512)S(1)} %get-tuple-element.418, f32[1024,400]{1,0:T(8,128)S(1)} %copy-done.6, s32[]{:T(128)S(6)} %select_n.141), kind=kOutput, calls=%fused_computation.14.clone.1 | convolution fusion | flops 2458624000 | bytes 4700676 | tf_op jit(solution)/shard_map/while/body/eval_jaxpr/dot_general | solution.py:53
  177.3 10.1 %scatter_fusion = f32[1024,400]{1,0:T(8,128)} fusion(f32[1024,400]{1,0:T(8,128)} %get-tuple-element.438, s32[1000]{0:T(1024)S(1)} %bitcast.49, f32[1000,400]{1,0:T(8,128)} %fusion.49), kind=kCustom, calls=%fused_computation.6.clone.1 | custom fusion | flops 400000 | bytes 4804000 | tf_op jit(solution)/shard_map/while/body/eval_jaxpr/scatter-add | solution.py:109
  187.6 3.0 copy.55
  190.5 2.0 multiply_add_fusion
  193.4 2.9 multiply_add_fusion.1
  196.3 8.3 %scatter_custom_fusion.1 = f32[1024,400]{1,0:T(8,128)S(1)} fusion(s32[1024]{0:T(1024)S(1)} %get-tuple-element.348, f32[1024,200]{1,0:T(8,128)} %get-tuple-element.333, f32[]{:T(128)} %constant.131, f32[1024,200]{1,0:T(8,128)} %get-tuple-element.334, f32[]{:T(128)} %constant.118.clone.1), kind=kCustom, calls=%fused_computation.39 | custom fusion | flops 819200 | bytes 3276808 | tf_op jit(solution)/shard_map/scatter-add | solution.py:124
  206.3 4.4 all-to-all-start.2
  210.8 8.5 %scatter_custom_fusion.3 = f32[1024,400]{1,0:T(8,128)S(1)} fusion(f32[1024,400]{1,0:T(8,128)S(1)} %copy-done, s32[1024]{0:T(1024)S(1)} %get-tuple-element.345, f32[1024]{0:T(1024)S(1)} %get-tuple-element.249, f32[1024,200]{1,0:T(8,128)} %copy-done.10, f32[1024,200]{1,0:T(8,128)S(1)} %get-tuple-element.331), kind=kCustom, calls=%fused_computation.47 | custom fusion | flops 1228800 | bytes 3510272 | tf_op jit(solution)/shard_map/scatter-add | solution.py:120
  219.4 1.9 copy.69
  221.3 9.3 %scatter_custom_fusion.5 = f32[1345,400]{1,0:T(8,128)} fusion(s32[1024]{0:T(1024)S(1)} %get-tuple-element.343, f32[1024,200]{1,0:T(8,128)} %get-tuple-element.328, f32[]{:T(128)} %constant.131, f32[1024,200]{1,0:T(8,128)S(1)} %copy-done.14, f32[]{:T(128)} %constant.118.clone.1), kind=kCustom, calls=%fused_computation.43 | custom fusion | flops 819200 | bytes 4019784 | tf_op jit(solution)/shard_map/scatter-add | solution.py:129
  233.5 3.5 collective-permute-start.1
  237.6 2.5 collective-permute-start.4
  240.0 5.6 %collective-permute-done.1 = f32[1,128,400]{1,0,2:T(1,128)S(1)} collective-permute-done((f32[1,128,400]{1,0,2:T(1,128)S(1)}, f32[1,128,400]{1,0,2:T(1,128)S(1)}, u32[]{:S(2)}, u32[]{:S(2)}) %collective-permute-start.1) | collective-permute-done | bytes 204832 | tf_op jit(solution)/shard_map/ppermute | solution.py:155
  245.6 11.1 %collective-permute-done.2 = f32[1,128,400]{1,0,2:T(1,128)S(1)} collective-permute-done((f32[1,128,400]{1,0,2:T(1,128)S(1)}, f32[1,128,400]{1,0,2:T(1,128)S(1)}, u32[]{:S(2)}, u32[]{:S(2)}) %collective-permute-start.2) | collective-permute-done | bytes 204832 | tf_op jit(solution)/shard_map/ppermute | solution.py:155
  256.7 23.2 %collective-permute-start.7 = (f32[1,128,400]{1,0,2:T(1,128)S(1)}, f32[1,128,400]{1,0,2:T(1,128)S(1)}, u32[]{:S(2)}, u32[]{:S(2)}) collective-permute-start(f32[1,128,400]{1,0,2:T(1,128)S(1)} %get-tuple-element.336), channel_id=1, source_target_pairs={{0,1},{1,2},{2,3},{3,4},{4,5},{5,6},{6,7},{7,0},{8,9},{9,10},{10,1... | collective-permute-start | bytes 614408 | tf_op jit(solution)/shard_map/ppermute | solution.py:155
  280.0 18.6 %collective-permute-done.4 = f32[1,128,400]{1,0,2:T(1,128)S(1)} collective-permute-done((f32[1,128,400]{1,0,2:T(1,128)S(1)}, f32[1,128,400]{1,0,2:T(1,128)S(1)}, u32[]{:S(2)}, u32[]{:S(2)}) %collective-permute-start.4) | collective-permute-done | bytes 204832 | tf_op jit(solution)/shard_map/ppermute | solution.py:155
  298.6 6.1 %concatenate.17 = f32[8,128,400]{1,0,2:T(8,128)S(1)} concatenate(f32[1,128,400]{1,0,2:T(1,128)S(1)} %collective-permute-done.1, f32[1,128,400]{1,0,2:T(1,128)S(1)} %collective-permute-done.2, f32[1,128,400]{1,0,2:T(1,128)S(1)} %collective-permute-done.3, f32[1,128,400]{1,0,2:T(1,128)S(1)} %collective-permute-done.4, f32[1,128,400]{1,0,2:T(1,128)S(1)} %collective-permute-done.5, ...), dimensions={0} | concatenate | bytes 3276800 | tf_op jit(solution)/shard_map/concatenate | solution.py:157
  306.6 2.4 collective-permute-start.8
  309.0 110.6 %all-reduce.2.cloned.1.call-done = f32[1345,400]{1,0:T(8,128)} async-done(((f32[1345,400]{1,0:T(8,128)}), f32[1345,400]{1,0:T(8,128)}) %all-reduce.2.cloned.1.call-update) | async-done | bytes 2152016 | tf_op jit(solution)/shard_map/psum | solution.py:131
  419.6 2.1 multiply_reduce_fusion.1
  421.7 3.8 divide_subtract_fusion
  425.6 3.5 copy.66
  429.1 2.8 copy.70
  431.9 1.8 copy.68
  433.7 6.8 %scatter_custom_fusion.2 = f32[512,400]{1,0:T(8,128)S(1)} fusion(s32[1024]{0:T(1024)S(1)} %bitcast.53, f32[1024,400]{1,0:T(8,128)S(1)} %bitcast.47, f32[]{:T(128)} %constant.118.clone.1), kind=kCustom, calls=%fused_computation.63 | custom fusion | flops 409600 | bytes 819204 | tf_op jit(solution)/shard_map/scatter-add | solution.py:142
  440.6 7.7 %scatter_fusion.1 = f32[512,400]{1,0:T(8,128)S(1)} fusion(f32[512,400]{1,0:T(8,128)S(1)} %scatter_custom_fusion.2, s32[1024]{0:T(1024)S(1)} %bitcast.50, f32[1024,400]{1,0:T(8,128)} %bitcast.43), kind=kCustom, calls=%fused_computation.10 | custom fusion | flops 409600 | bytes 4919296 | tf_op jit(solution)/shard_map/scatter-add | solution.py:162
  (112 shorter events, 31.8 us)
Async XLA Ops:
  8.6 12.5 %copy-start.1 = (f32[512,400]{1,0:T(8,128)}, f32[512,400]{1,0:T(8,128)S(1)}, u32[]{:S(2)}) copy-start(f32[512,400]{1,0:T(8,128)S(1)} %copy.63) | copy-start | bytes 2457604
  14.6 6.5 %copy-start.17 = (s32[1,8,128]{2,1,0:T(8,128)S(1)}, s32[1,8,128]{2,1,0:T(8,128)}, u32[]{:S(2)}) copy-start(s32[1,8,128]{2,1,0:T(8,128)} %param.20) | copy-start | bytes 12292
  14.6 50.3 %all-to-all-start = ((f32[8,128,400]{1,2,0:T(8,128)}), f32[8,128,400]{1,2,0:T(8,128)}, u32[]{:S(2)}, u32[]{:S(2)}) async-start(f32[8,128,400]{1,2,0:T(8,128)} %copy.48), calls=%async_computation | async-start | bytes 3276800 | tf_op jit(solution)/shard_map/all_to_all | solution.py:82
  26.4 38.5 %collective-permute-start = (f32[8,128,400]{1,2,0:T(8,128)}, f32[8,128,400]{1,2,0:T(8,128)}, u32[]{:S(2)}, u32[]{:S(2)}) collective-permute-start(f32[8,128,400]{1,2,0:T(8,128)} %copy.52), channel_id=1, source_target_pairs={{0,24},{8,0},{16,8},{24,16},{1,25},{9,1},{17,9},{25,17},{2,26},{10... | collective-permute-start | bytes 4915208 | tf_op jit(solution)/shard_map/ppermute | solution.py:12
  64.9 44.0 %all-to-all-start.1 = ((f32[8,128,400]{1,2,0:T(8,128)}), f32[8,128,400]{1,2,0:T(8,128)}, u32[]{:S(2)}, u32[]{:S(2)}) async-start(f32[8,128,400]{1,2,0:T(8,128)} %collective-permute-done), calls=%async_computation.1 | async-start | bytes 3276800 | tf_op jit(solution)/shard_map/all_to_all | solution.py:87
  69.6 3.2 copy-start.20
  72.2 5.6 %copy-start.4 = (f32[1345,400]{1,0:T(8,128)}, f32[1345,400]{1,0:T(8,128)S(1)}, u32[]{:S(2)}) copy-start(f32[1345,400]{1,0:T(8,128)S(1)} %copy.50) | copy-start | bytes 6456004
  72.9 4.9 %copy-start.21 = (s32[1024]{0:T(1024)S(1)}, s32[1024]{0:T(1024)}, u32[]{:S(2)}) copy-start(s32[1024]{0:T(1024)} %param.21) | copy-start | bytes 12292
  72.9 4.9 %copy-start.22 = (s32[1024]{0:T(1024)S(1)}, s32[1024]{0:T(1024)}, u32[]{:S(2)}) copy-start(s32[1024]{0:T(1024)} %param.23) | copy-start | bytes 12292
  87.8 1.0 copy-start.10
  115.7 2.9 copy-start.15
  125.8 6.1 %copy-start.11 = (f32[1024,400]{0,1:T(8,128)S(1)}, f32[1024,400]{0,1:T(8,128)}, u32[]{:S(2)}) copy-start(f32[1024,400]{0,1:T(8,128)} %get-tuple-element.437) | copy-start | bytes 4915204 | tf_op jit(solution)/shard_map/while
  131.3 1.6 copy-start.3
  132.8 5.4 %copy-start.6 = (f32[1024,400]{1,0:T(8,128)S(1)}, f32[1024,400]{1,0:T(8,128)}, u32[]{:S(2)}) copy-start(f32[1024,400]{1,0:T(8,128)} %get-tuple-element.453) | copy-start | bytes 4915204 | tf_op jit(solution)/shard_map/while
  137.1 1.2 copy-start.12
  159.9 6.1 %copy-start.11 = (f32[1024,400]{0,1:T(8,128)S(1)}, f32[1024,400]{0,1:T(8,128)}, u32[]{:S(2)}) copy-start(f32[1024,400]{0,1:T(8,128)} %get-tuple-element.437) | copy-start | bytes 4915204 | tf_op jit(solution)/shard_map/while
  165.4 1.6 copy-start.3
  166.9 5.4 %copy-start.6 = (f32[1024,400]{1,0:T(8,128)S(1)}, f32[1024,400]{1,0:T(8,128)}, u32[]{:S(2)}) copy-start(f32[1024,400]{1,0:T(8,128)} %get-tuple-element.453) | copy-start | bytes 4915204 | tf_op jit(solution)/shard_map/while
  171.2 1.2 copy-start.12
  187.6 5.0 %copy-start.23 = (f32[1024]{0:T(1024)}, f32[1024]{0:T(1024)S(1)}, u32[]{:S(2)}) copy-start(f32[1024]{0:T(1024)S(1)} %get-tuple-element.301) | copy-start | bytes 12292
  187.6 3.0 copy-start.7
  190.5 2.2 copy-start.8
  190.5 2.9 copy-start.9
  206.3 4.5 copy-start
  206.3 225.5 %all-to-all-start.2 = ((f32[8,128,400]{1,2,0:T(8,128)}), f32[8,128,400]{1,2,0:T(8,128)}, u32[]{:S(2)}, u32[]{:S(2)}) async-start(f32[8,128,400]{1,2,0:T(8,128)} %copy.56), calls=%async_computation.2 | async-start | bytes 3276800 | tf_op jit(solution)/shard_map/all_to_all | solution.py:132
  210.8 208.9 %all-reduce.2.cloned.1.call-start = ((), (), s32[]{:S(2)}) async-start(), calls=%async_computation.3 | async-start | bytes 5537792 | tf_op jit(solution)/shard_map/psum | solution.py:131
  219.4 1.9 copy-start.14
  230.6 1.4 copy-start.13
  233.5 12.1 %collective-permute-start.1 = (f32[1,128,400]{1,0,2:T(1,128)S(1)}, f32[1,128,400]{1,0,2:T(1,128)S(1)}, u32[]{:S(2)}, u32[]{:S(2)}) collective-permute-start(f32[1,128,400]{1,0,2:T(1,128)S(1)} %get-tuple-element.342), channel_id=1, source_target_pairs={{0,7},{1,0},{2,1},{3,2},{4,3},{5,4},{6,5},{7,6},{8,15},{9,8},{10,9... | collective-permute-start | bytes 614408 | tf_op jit(solution)/shard_map/ppermute | solution.py:155
  237.0 19.7 %collective-permute-start.2 = (f32[1,128,400]{1,0,2:T(1,128)S(1)}, f32[1,128,400]{1,0,2:T(1,128)S(1)}, u32[]{:S(2)}, u32[]{:S(2)}) collective-permute-start(f32[1,128,400]{1,0,2:T(1,128)S(1)} %get-tuple-element.341), channel_id=1, source_target_pairs={{0,6},{1,7},{2,0},{3,1},{4,2},{5,3},{6,4},{7,5},{8,14},{9,15},{10,... | collective-permute-start | bytes 614408 | tf_op jit(solution)/shard_map/ppermute | solution.py:155
  237.5 42.4 %collective-permute-start.3 = (f32[1,128,400]{1,0,2:T(1,128)S(1)}, f32[1,128,400]{1,0,2:T(1,128)S(1)}, u32[]{:S(2)}, u32[]{:S(2)}) collective-permute-start(f32[1,128,400]{1,0,2:T(1,128)S(1)} %get-tuple-element.340), channel_id=1, source_target_pairs={{0,5},{1,6},{2,7},{3,0},{4,1},{5,2},{6,3},{7,4},{8,13},{9,14},{10,... | collective-permute-start | bytes 614408 | tf_op jit(solution)/shard_map/ppermute | solution.py:155
  237.6 61.0 %collective-permute-start.4 = (f32[1,128,400]{1,0,2:T(1,128)S(1)}, f32[1,128,400]{1,0,2:T(1,128)S(1)}, u32[]{:S(2)}, u32[]{:S(2)}) collective-permute-start(f32[1,128,400]{1,0,2:T(1,128)S(1)} %get-tuple-element.339), channel_id=1, source_target_pairs={{0,4},{1,5},{2,6},{3,7},{4,0},{5,1},{6,2},{7,3},{8,12},{9,13},{10,... | collective-permute-start | bytes 614408 | tf_op jit(solution)/shard_map/ppermute | solution.py:155
  240.0 58.5 %collective-permute-start.5 = (f32[1,128,400]{1,0,2:T(1,128)S(1)}, f32[1,128,400]{1,0,2:T(1,128)S(1)}, u32[]{:S(2)}, u32[]{:S(2)}) collective-permute-start(f32[1,128,400]{1,0,2:T(1,128)S(1)} %get-tuple-element.338), channel_id=1, source_target_pairs={{0,3},{1,4},{2,5},{3,6},{4,7},{5,0},{6,1},{7,2},{8,11},{9,12},{10,... | collective-permute-start | bytes 614408 | tf_op jit(solution)/shard_map/ppermute | solution.py:155
  245.6 52.9 %collective-permute-start.6 = (f32[1,128,400]{1,0,2:T(1,128)S(1)}, f32[1,128,400]{1,0,2:T(1,128)S(1)}, u32[]{:S(2)}, u32[]{:S(2)}) collective-permute-start(f32[1,128,400]{1,0,2:T(1,128)S(1)} %get-tuple-element.337), channel_id=1, source_target_pairs={{0,2},{1,3},{2,4},{3,5},{4,6},{5,7},{6,0},{7,1},{8,10},{9,11},{10,... | collective-permute-start | bytes 614408 | tf_op jit(solution)/shard_map/ppermute | solution.py:155
  256.7 41.9 %collective-permute-start.7 = (f32[1,128,400]{1,0,2:T(1,128)S(1)}, f32[1,128,400]{1,0,2:T(1,128)S(1)}, u32[]{:S(2)}, u32[]{:S(2)}) collective-permute-start(f32[1,128,400]{1,0,2:T(1,128)S(1)} %get-tuple-element.336), channel_id=1, source_target_pairs={{0,1},{1,2},{2,3},{3,4},{4,5},{5,6},{6,7},{7,0},{8,9},{9,10},{10,1... | collective-permute-start | bytes 614408 | tf_op jit(solution)/shard_map/ppermute | solution.py:155
  305.1 3.8 copy-start.16
  305.2 3.8 copy-start.18
  306.6 115.1 %copy-start.19 = (f32[1345]{0:T(1024)S(1)}, f32[1345]{0:T(1024)}, u32[]{:S(2)}) copy-start(f32[1345]{0:T(1024)} %param.18) | copy-start | bytes 16144
  306.6 115.1 %copy-start.5 = (f32[1345,400]{1,0:T(8,128)S(1)}, f32[1345,400]{1,0:T(8,128)}, u32[]{:S(2)}) copy-start(f32[1345,400]{1,0:T(8,128)} %copy-done.4) | copy-start | bytes 6456004
  306.6 122.4 %collective-permute-start.8 = (f32[8,128,400]{1,2,0:T(8,128)}, f32[8,128,400]{1,2,0:T(8,128)}, u32[]{:S(2)}, u32[]{:S(2)}) collective-permute-start(f32[8,128,400]{1,2,0:T(8,128)} %copy.60), channel_id=1, source_target_pairs={{0,8},{8,16},{16,24},{24,0},{1,9},{9,17},{17,25},{25,1},{2,10},{10... | collective-permute-start | bytes 4915208 | tf_op jit(solution)/shard_map/ppermute | solution.py:12
  440.6 7.9 %copy-start.24 = (f32[512]{0:T(512)S(1)}, f32[512]{0:T(512)}, u32[]{:S(2)}) copy-start(f32[512]{0:T(512)} %param.16) | copy-start | bytes 6148
  440.6 7.9 %copy-start.2 = (f32[512,400]{1,0:T(8,128)S(1)}, f32[512,400]{1,0:T(8,128)}, u32[]{:S(2)}) copy-start(f32[512,400]{1,0:T(8,128)} %copy-done.1) | copy-start | bytes 2457604
Sparse Core Ops, SparseCore 0:
  230.7 188.8 all-reduce.1
